TPU v7x, 32 devices: a whole 2x2x4 slice. The times are simulated.
32 devices in a mesh: groups: 2 (over x), segment: 2 (over core), block: 8 (over z, y).
Axes of the slice: x: 2, y: 2, z: 4, core: 2. Of those that a mesh axis runs over, the one named last changes fastest.
Arguments:
- tokens: float32 [1024, 16384], P(('groups', 'segment'), 'block'), parts along dimension 0, may hold values from -32 to 32
- gains: float32 [2, 2, 16384], P('segment', None, 'block'), may hold values from 0.1 to 1.9
- right_factors: float32 [2, 2, 128, 128, 128], P('segment', None, 'block'), may hold values from -0.5 to 0.5
- left_factors: float32 [2, 2, 128, 128, 128], P('segment', None, 'block'), may hold values from -0.5 to 0.5
Outputs:
- output: float32 [1024, 16384], P(('groups', 'segment'), 'block'), parts along dimension 0
There are 2 independent parts, one for each index of `groups`. A program takes and returns all parts, laid end to end along the dimension named above; an argument that names none is the same for every part. Nothing has to cross between parts.
All inputs are finite; a program needn't handle non-finite values.
Results may differ from a plain program's by a relative error of at most 0.0003.
Values sent between devices are 32-bit elements; how exact they have to be, the bound alone decides.
A program may use at most 64 MiB of HBM per device.

v0:
```python
import jax
import jax.numpy as jnp
from jax import lax
from jax.sharding import PartitionSpec as P

D = 16384


epsilon = 1e-06
exact = lax.Precision.HIGHEST


def shifted(block, axis, distance):
    devices = range(lax.axis_size(axis))
    route = [((i - distance) % len(devices), i) for i in devices]
    return lax.ppermute(block, axis, route)


def apply_layer(current, gain_row, right_part, left_part):
    blocks_here = right_part.shape[0]
    block_size = right_part.shape[1]
    width_here, token_count = current.shape
    partial_squares = jnp.sum(current * current, axis=0)
    sum_squares = lax.psum(partial_squares, "block")
    normed = current * lax.rsqrt(sum_squares / D + epsilon)[None, :] * gain_row[:, None]
    inner = jnp.einsum(
        "bit,bij->bjt",
        normed.reshape(blocks_here, block_size, token_count),
        right_part,
        precision=exact,
    )
    combined = jnp.einsum(
        "bjt,jbc->cjt",
        lax.all_to_all(inner, "block", split_axis=1, concat_axis=0, tiled=True),
        left_part,
        precision=exact,
    )
    mixed = lax.all_to_all(combined, "block", split_axis=0, concat_axis=1, tiled=True)
    return current + mixed.reshape(width_here, token_count) * jax.nn.silu(normed)


def body(tokens, gains, right_factors, left_factors):
    current = tokens.T
    rounds = right_factors.shape[1]
    layer_count = 2 * rounds
    segment_index = lax.axis_index("segment")
    for moment in range(layer_count + 1):
        holding = jnp.remainder(moment - segment_index, 2)
        layer_index = moment - holding
        active = (layer_index >= 0) & (layer_index < layer_count)
        round_index = jnp.clip(layer_index // 2, 0, rounds - 1)
        gain_row = lax.dynamic_index_in_dim(gains[0], round_index, 0, keepdims=False)
        right_part = lax.dynamic_index_in_dim(right_factors[0], round_index, 0, keepdims=False)
        left_part = lax.dynamic_index_in_dim(left_factors[0], round_index, 0, keepdims=False)
        updated = apply_layer(current, gain_row, right_part, left_part)
        current = jnp.where(active, updated, current)
        if moment < layer_count:
            current = shifted(current, "segment", 1)
    return current.T


def solution(mesh):
    placed = (
        P(("groups", "segment"), "block"),
        P("segment", None, "block"),
        P("segment", None, "block", None, None),
        P("segment", None, "block", None, None),
    )
    return jax.shard_map(
        body,
        mesh=mesh,
        in_specs=placed,
        out_specs=P(("groups", "segment"), "block"),
        check_vma=False,
    )
```

profile of v0, /device:TPU:27, one launch (start us, length us, event | category | flops | bytes accessed | tf_op | source)
XLA Modules:
  0.0 693.8 jit_solution(2861334446131708136)
XLA Ops:
  0.0 3.0 copy.79
  3.0 1.9 fusion.1
  4.9 13.4 %psum.35 = f32[256]{0:T(256)S(1)} all-reduce(f32[256]{0:T(256)S(1)} %fusion.1), channel_id=1, replica_groups=mesh['groups'=2,'segment'=2,'block'=8] {'block'}, use_global_device_ids=true, to_apply=%region_1.2 | all-reduce | flops 256 | bytes 2048 | tf_op jit(solution)/shard_map/psum | solution.py:24
  18.4 1.9 fusion.2
  20.3 2.0 fusion.16
  22.3 1.2 copy.82
  23.5 51.3 %all_to_all.165 = f32[16,128,256]{2,0,1:T(8,128)S(1)} all-to-all(f32[16,128,256]{2,0,1:T(8,128)S(1)} %copy.82), channel_id=1, replica_groups=mesh['groups'=2,'segment'=2,'block'=8] {'block'}, dimensions={1} | all-to-all | bytes 4194304 | tf_op jit(solution)/shard_map/all_to_all | solution.py:34
  75.1 1.3 copy-done.10
  76.4 2.1 convolution_bitcast_fusion.4
  78.5 2.5 copy.84
  81.0 6.3 all-to-all-start.1
  87.3 46.1 %all-to-all-done.1 = f32[128,16,256]{2,1,0:T(8,128)} async-done(((f32[128,16,256]{2,1,0:T(8,128)}), f32[128,16,256]{2,1,0:T(8,128)}, u32[]{:S(2)}, u32[]{:S(2)}) %all-to-all-start.1) | async-done | bytes 2097184 | tf_op jit(solution)/shard_map/all_to_all | solution.py:38
  133.4 1.9 copy.85
  137.4 3.8 collective-permute-done
  141.2 1.3 copy-done.4
  142.8 13.7 %psum.36 = f32[256]{0:T(256)S(1)} all-reduce(f32[256]{0:T(256)S(1)} %multiply_reduce_fusion.3), channel_id=1, replica_groups=mesh['groups'=2,'segment'=2,'block'=8] {'block'}, use_global_device_ids=true, to_apply=%region_3.4 | all-reduce | flops 256 | bytes 2048 | tf_op jit(solution)/shard_map/psum | solution.py:24
  156.5 1.9 multiply_multiply_fusion.3
  158.4 2.0 fusion.13
  160.4 1.2 copy.88
  161.6 52.0 %all_to_all.166 = f32[16,128,256]{2,0,1:T(8,128)S(1)} all-to-all(f32[16,128,256]{2,0,1:T(8,128)S(1)} %copy.88), channel_id=1, replica_groups=mesh['groups'=2,'segment'=2,'block'=8] {'block'}, dimensions={1} | all-to-all | bytes 4194304 | tf_op jit(solution)/shard_map/all_to_all | solution.py:34
  213.9 1.3 copy-done.11
  215.2 2.1 convolution_bitcast_fusion.3
  217.3 2.5 copy.90
  219.8 5.7 all-to-all-start.3
  225.5 46.1 %all-to-all-done.3 = f32[128,16,256]{2,1,0:T(8,128)} async-done(((f32[128,16,256]{2,1,0:T(8,128)}), f32[128,16,256]{2,1,0:T(8,128)}, u32[]{:S(2)}, u32[]{:S(2)}) %all-to-all-start.3) | async-done | bytes 2097184 | tf_op jit(solution)/shard_map/all_to_all | solution.py:38
  271.6 1.9 copy.91
  275.6 3.8 collective-permute-done.1
  279.4 1.3 copy-done.6
  281.0 13.9 %psum.37 = f32[256]{0:T(256)S(1)} all-reduce(f32[256]{0:T(256)S(1)} %multiply_reduce_fusion.2), channel_id=1, replica_groups=mesh['groups'=2,'segment'=2,'block'=8] {'block'}, use_global_device_ids=true, to_apply=%region_5.6 | all-reduce | flops 256 | bytes 2048 | tf_op jit(solution)/shard_map/psum | solution.py:24
  294.8 1.9 multiply_multiply_fusion.2
  296.8 2.0 fusion.10
  300.0 52.0 %all_to_all.167 = f32[16,128,256]{2,0,1:T(8,128)S(1)} all-to-all(f32[16,128,256]{2,0,1:T(8,128)S(1)} %copy.94), channel_id=1, replica_groups=mesh['groups'=2,'segment'=2,'block'=8] {'block'}, dimensions={1} | all-to-all | bytes 4194304 | tf_op jit(solution)/shard_map/all_to_all | solution.py:34
  352.2 1.3 copy-done.12
  353.6 2.1 convolution_bitcast_fusion.2
  355.7 2.5 copy.96
  358.2 5.7 all-to-all-start.5
  363.9 46.1 %all-to-all-done.5 = f32[128,16,256]{2,1,0:T(8,128)} async-done(((f32[128,16,256]{2,1,0:T(8,128)}), f32[128,16,256]{2,1,0:T(8,128)}, u32[]{:S(2)}, u32[]{:S(2)}) %all-to-all-start.5) | async-done | bytes 2097184 | tf_op jit(solution)/shard_map/all_to_all | solution.py:38
  410.0 1.9 copy.97
  414.0 3.8 collective-permute-done.2
  417.8 1.3 copy-done.8
  419.4 13.6 %psum.38 = f32[256]{0:T(256)S(1)} all-reduce(f32[256]{0:T(256)S(1)} %multiply_reduce_fusion.1), channel_id=1, replica_groups=mesh['groups'=2,'segment'=2,'block'=8] {'block'}, use_global_device_ids=true, to_apply=%region_7.8 | all-reduce | flops 256 | bytes 2048 | tf_op jit(solution)/shard_map/psum | solution.py:24
  433.0 1.9 multiply_multiply_fusion.1
  434.9 2.0 fusion.7
  438.1 52.0 %all_to_all.168 = f32[16,128,256]{2,0,1:T(8,128)S(1)} all-to-all(f32[16,128,256]{2,0,1:T(8,128)S(1)} %copy.100), channel_id=1, replica_groups=mesh['groups'=2,'segment'=2,'block'=8] {'block'}, dimensions={1} | all-to-all | bytes 4194304 | tf_op jit(solution)/shard_map/all_to_all | solution.py:34
  490.4 1.3 copy-done.13
  491.7 2.1 convolution_bitcast_fusion.1
  493.8 2.5 copy.102
  496.3 5.7 all-to-all-start.7
  502.0 46.1 %all-to-all-done.7 = f32[128,16,256]{2,1,0:T(8,128)} async-done(((f32[128,16,256]{2,1,0:T(8,128)}), f32[128,16,256]{2,1,0:T(8,128)}, u32[]{:S(2)}, u32[]{:S(2)}) %all-to-all-start.7) | async-done | bytes 2097184 | tf_op jit(solution)/shard_map/all_to_all | solution.py:38
  548.1 1.9 copy.103
  552.1 3.8 collective-permute-done.3
  555.9 1.3 copy-done.2
  557.5 13.7 %psum.39 = f32[256]{0:T(256)S(1)} all-reduce(f32[256]{0:T(256)S(1)} %multiply_reduce_fusion), channel_id=1, replica_groups=mesh['groups'=2,'segment'=2,'block'=8] {'block'}, use_global_device_ids=true, to_apply=%region_9.10 | all-reduce | flops 256 | bytes 2048 | tf_op jit(solution)/shard_map/psum | solution.py:24
  571.2 1.9 multiply_multiply_fusion
  573.1 2.0 fusion.4
  576.3 52.0 %all_to_all.169 = f32[16,128,256]{2,0,1:T(8,128)S(1)} all-to-all(f32[16,128,256]{2,0,1:T(8,128)S(1)} %copy.106), channel_id=1, replica_groups=mesh['groups'=2,'segment'=2,'block'=8] {'block'}, dimensions={1} | all-to-all | bytes 4194304 | tf_op jit(solution)/shard_map/all_to_all | solution.py:34
  628.6 1.3 copy-done.14
  629.9 2.1 convolution_bitcast_fusion
  632.0 2.5 copy.108
  634.5 5.7 all-to-all-start.9
  640.2 46.1 %all-to-all-done.9 = f32[128,16,256]{2,1,0:T(8,128)} async-done(((f32[128,16,256]{2,1,0:T(8,128)}), f32[128,16,256]{2,1,0:T(8,128)}, u32[]{:S(2)}, u32[]{:S(2)}) %all-to-all-start.9) | async-done | bytes 2097184 | tf_op jit(solution)/shard_map/all_to_all | solution.py:38
  686.3 1.9 copy.109
  688.5 2.2 fusion
  690.7 2.9 copy.110
  (49 shorter events, 14.7 us)
Async XLA Ops:
  0.0 20.3 %copy-start = (f32[1,2,16,128,128]{4,3,2,1,0:T(8,128)S(1)}, f32[1,2,16,128,128]{4,3,2,1,0:T(8,128)}, u32[]{:S(2)}) copy-start(f32[1,2,16,128,128]{4,3,2,1,0:T(8,128)} %param.6) | copy-start | bytes 6291460
  3.0 15.3 %copy-start.15 = (f32[1,2,2048]{2,1,0:T(2,128)S(1)}, f32[1,2,2048]{2,1,0:T(2,128)}, u32[]{:S(2)}) copy-start(f32[1,2,2048]{2,1,0:T(2,128)} %param.5) | copy-start | bytes 49156
  74.8 1.6 copy-start.10
  81.0 52.4 %all-to-all-start.1 = ((f32[128,16,256]{2,1,0:T(8,128)}), f32[128,16,256]{2,1,0:T(8,128)}, u32[]{:S(2)}, u32[]{:S(2)}) async-start(f32[128,16,256]{2,1,0:T(8,128)} %copy.84), calls=%async_computation.1 | async-start | bytes 4194304 | tf_op jit(solution)/shard_map/all_to_all | solution.py:38
  133.4 2.2 copy-start.1
  136.5 4.7 collective-permute-start
  141.2 1.3 copy-start.4
  213.6 1.6 copy-start.11
  219.8 51.8 %all-to-all-start.3 = ((f32[128,16,256]{2,1,0:T(8,128)}), f32[128,16,256]{2,1,0:T(8,128)}, u32[]{:S(2)}, u32[]{:S(2)}) async-start(f32[128,16,256]{2,1,0:T(8,128)} %copy.90), calls=%async_computation.3 | async-start | bytes 4194304 | tf_op jit(solution)/shard_map/all_to_all | solution.py:38
  271.6 2.2 copy-start.5
  274.7 4.7 collective-permute-start.1
  279.4 1.3 copy-start.6
  352.0 1.6 copy-start.12
  358.2 51.8 %all-to-all-start.5 = ((f32[128,16,256]{2,1,0:T(8,128)}), f32[128,16,256]{2,1,0:T(8,128)}, u32[]{:S(2)}, u32[]{:S(2)}) async-start(f32[128,16,256]{2,1,0:T(8,128)} %copy.96), calls=%async_computation.5 | async-start | bytes 4194304 | tf_op jit(solution)/shard_map/all_to_all | solution.py:38
  410.0 2.2 copy-start.7
  413.1 4.7 collective-permute-start.2
  417.8 1.3 copy-start.8
  490.2 1.6 copy-start.13
  496.3 51.8 %all-to-all-start.7 = ((f32[128,16,256]{2,1,0:T(8,128)}), f32[128,16,256]{2,1,0:T(8,128)}, u32[]{:S(2)}, u32[]{:S(2)}) async-start(f32[128,16,256]{2,1,0:T(8,128)} %copy.102), calls=%async_computation.7 | async-start | bytes 4194304 | tf_op jit(solution)/shard_map/all_to_all | solution.py:38
  548.1 2.2 copy-start.9
  551.2 4.7 collective-permute-start.3
  555.9 1.3 copy-start.2
  628.3 1.6 copy-start.14
  634.5 51.8 %all-to-all-start.9 = ((f32[128,16,256]{2,1,0:T(8,128)}), f32[128,16,256]{2,1,0:T(8,128)}, u32[]{:S(2)}, u32[]{:S(2)}) async-start(f32[128,16,256]{2,1,0:T(8,128)} %copy.108), calls=%async_computation.9 | async-start | bytes 4194304 | tf_op jit(solution)/shard_map/all_to_all | solution.py:38
  686.3 2.2 copy-start.3
where the time goes:
time: 706 us; the launch traced here: 694 us
  blocking collectives  328 us (46%)
  waiting for transfers between devices  245 us (35%)
  local copies, waits for them, and re-layouts  48.9 us (7%)
  starting transfers between devices  32.9 us (5%)
  matrix products  20.2 us (3%)
  other arithmetic  18.4 us (3%)
    all_to_all x5, blocking collectives, apply_layer(): lax.all_to_all(inner, 'block', split_axis=1, concat_axis=0, tiled=True)  259 us
    all_to_all x5, waiting for transfers between devices, apply_layer(): lax.all_to_all(combined, 'block', split_axis=0, concat_axis=1, tiled=True)  230 us
    psum x5, blocking collectives, apply_layer(): sum_squares = lax.psum(partial_squares, 'block')  68.2 us
    all_to_all x5, starting transfers between devices, apply_layer(): lax.all_to_all(combined, 'block', split_axis=0, concat_axis=1, tiled=True)  29.2 us
    unnamed x33, local copies, waits for them, and re-layouts  16.5 us
    ppermute x4, waiting for transfers between devices, shifted(): return lax.ppermute(block, axis, route)  15.1 us
  transfers between devices with their start and end apart: 9, of which 9 were waited for; matrix products, arithmetic and copies ran while one was open for 0% of the time, Pallas kernels for 0%

commit v1 on v0

--- a/solution.py
+++ b/solution.py
@@ -7,7 +7,7 @@
 
 
 epsilon = 1e-06
-exact = lax.Precision.HIGHEST
+exact = lax.Precision.HIGH
 
 
 def shifted(block, axis, distance):
@@ -21,7 +21,9 @@
     block_size = right_part.shape[1]
     width_here, token_count = current.shape
     partial_squares = jnp.sum(current * current, axis=0)
-    sum_squares = lax.psum(partial_squares, "block")
+    devices = lax.axis_size("block")
+    copies = jnp.broadcast_to(partial_squares, (devices, token_count))
+    sum_squares = lax.all_to_all(copies, "block", 0, 0, tiled=True).sum(axis=0)
     normed = current * lax.rsqrt(sum_squares / D + epsilon)[None, :] * gain_row[:, None]
     inner = jnp.einsum(
         "bit,bij->bjt",
@@ -42,20 +44,16 @@
 def body(tokens, gains, right_factors, left_factors):
     current = tokens.T
     rounds = right_factors.shape[1]
-    layer_count = 2 * rounds
     segment_index = lax.axis_index("segment")
-    for moment in range(layer_count + 1):
-        holding = jnp.remainder(moment - segment_index, 2)
-        layer_index = moment - holding
-        active = (layer_index >= 0) & (layer_index < layer_count)
-        round_index = jnp.clip(layer_index // 2, 0, rounds - 1)
-        gain_row = lax.dynamic_index_in_dim(gains[0], round_index, 0, keepdims=False)
-        right_part = lax.dynamic_index_in_dim(right_factors[0], round_index, 0, keepdims=False)
-        left_part = lax.dynamic_index_in_dim(left_factors[0], round_index, 0, keepdims=False)
-        updated = apply_layer(current, gain_row, right_part, left_part)
-        current = jnp.where(active, updated, current)
-        if moment < layer_count:
-            current = shifted(current, "segment", 1)
+    own = (gains[0], right_factors[0], left_factors[0])
+    other = [[shifted(part[r], "segment", 1) for part in own] for r in range(rounds)]
+    for layer_index in range(2 * rounds):
+        section, r = layer_index % 2, layer_index // 2
+        chosen = [
+            jnp.where(segment_index == section, mine[r], theirs)
+            for mine, theirs in zip(own, other[r])
+        ]
+        current = apply_layer(current, *chosen)
     return current.T
 
 

time: 706 us -> 515 us (0.73)
  waiting for transfers between devices: 245 us -> 134 us
  blocking collectives: 328 us -> 272 us
  local copies, waits for them, and re-layouts: 48.9 us -> 39.5 us
  matrix products: 20.2 us -> 12.1 us
  other arithmetic: 18.4 us -> 11.3 us
    all_to_all x5 -> x1, waiting for transfers between devices: 230 us -> 42.9 us  [apply_layer(): lax.all_to_all(combined, 'block', split_axis=0, concat_axis=1, tiled=True)]
    all_to_all x0 -> x5, blocking collectives: none -> 170 us  [the longest x3 153 us: apply_layer(): lax.all_to_all(combined, 'block', split_axis=0, concat_axis=1, tiled=True)]
    all_to_all x5 -> x2, blocking collectives: 259 us -> 102 us  [apply_layer(): lax.all_to_all(inner, 'block', split_axis=1, concat_axis=0, tiled=True)]
    all_to_all x0 -> x4, waiting for transfers between devices: none -> 91.4 us  [the longest x2 86.2 us: apply_layer(): lax.all_to_all(inner, 'block', split_axis=1, concat_axis=0, tiled=True)]
    psum x5 -> x0, blocking collectives: 68.2 us -> none  [apply_layer(): sum_squares = lax.psum(partial_squares, 'block')]
    all_to_all x0 -> x4, starting transfers between devices: none -> 25.6 us  [the longest x2 14 us: apply_layer(): lax.all_to_all(inner, 'block', split_axis=1, concat_axis=0, tiled=True)]
    all_to_all x5 -> x1, starting transfers between devices: 29.2 us -> 5.5 us  [apply_layer(): lax.all_to_all(combined, 'block', split_axis=0, concat_axis=1, tiled=True)]
    ppermute x4 -> x6, waiting for transfers between devices: 15.1 us -> 0.02 us  [shifted(): return lax.ppermute(block, axis, route)]
  transfers between devices with their start and end apart: 9 -> 11, of which waited for: 9 -> 5; matrix products, arithmetic and copies ran while one was open for 0% -> 3% of each run, Pallas kernels for 0% -> 0%
where the time goes in v1:
time: 515 us; the launch traced here: 509 us
  blocking collectives  272 us (53%)
  waiting for transfers between devices  134 us (26%)
  local copies, waits for them, and re-layouts  39.5 us (8%)
  starting transfers between devices  39.2 us (8%)
  matrix products  12.1 us (2%)
  other arithmetic  11.3 us (2%)
    all_to_all x3, blocking collectives, apply_layer(): lax.all_to_all(combined, 'block', split_axis=0, concat_axis=1, tiled=True)  153 us
    all_to_all x2, blocking collectives, apply_layer(): lax.all_to_all(inner, 'block', split_axis=1, concat_axis=0, tiled=True)  102 us
    all_to_all x2, waiting for transfers between devices, apply_layer(): lax.all_to_all(inner, 'block', split_axis=1, concat_axis=0, tiled=True)  86.2 us
    all_to_all x1, waiting for transfers between devices, apply_layer(): lax.all_to_all(combined, 'block', split_axis=0, concat_axis=1, tiled=True)  42.9 us
    all_to_all x2, blocking collectives, apply_layer(): sum_squares = lax.all_to_all(copies, 'block', 0, 0, tiled=True).sum(axis=0)  17.1 us
    all_to_all x2, starting transfers between devices, apply_layer(): lax.all_to_all(inner, 'block', split_axis=1, concat_axis=0, tiled=True)  14 us
    all_to_all x2, starting transfers between devices, apply_layer(): sum_squares = lax.all_to_all(copies, 'block', 0, 0, tiled=True).sum(axis=0)  11.6 us
    unnamed x21, local copies, waits for them, and re-layouts  10.7 us
  transfers between devices with their start and end apart: 11, of which 5 were waited for; matrix products, arithmetic and copies ran while one was open for 3% of the time, Pallas kernels for 0%

profile of v1, /device:TPU:27, one launch (start us, length us, event | category | flops | bytes accessed | tf_op | source)
XLA Modules:
  0.0 508.8 jit_solution(17633843209926145523)
XLA Ops:
  0.0 0.8 fusion.29
  0.8 0.7 collective-permute-start.2
  1.6 3.1 slice_bitcast_fusion
  4.7 1.9 copy.117
  6.6 0.3 fusion.4
  6.9 0.6 broadcast_in_dim.8
  7.5 5.5 %all-to-all-start = ((f32[8,1,256]{2,1,0:T(1,128)}), f32[8,1,256]{2,1,0:T(1,128)S(1)}, u32[]{:S(2)}, u32[]{:S(2)}) async-start(f32[8,1,256]{2,1,0:T(1,128)} %broadcast_in_dim.8), calls=%async_computation | async-start | bytes 16384 | tf_op jit(solution)/shard_map/all_to_all | solution.py:26
  13.0 2.6 all-to-all-done
  15.6 0.3 fusion.5
  16.0 1.2 copy-done.1
  17.2 1.2 fusion.15
  18.4 2.5 copy.120
  21.0 7.0 %all-to-all-start.1 = ((f32[16,128,256]{2,0,1:T(8,128)}), f32[16,128,256]{2,0,1:T(8,128)}, u32[]{:S(2)}, u32[]{:S(2)}) async-start(f32[16,128,256]{2,0,1:T(8,128)} %copy.120), calls=%async_computation.1 | async-start | bytes 4194304 | tf_op jit(solution)/shard_map/all_to_all | solution.py:36
  28.0 3.1 slice_bitcast_fusion.1
  31.1 2.2 collective-permute-start
  33.3 41.5 %all-to-all-done.1 = f32[16,128,256]{2,0,1:T(8,128)} async-done(((f32[16,128,256]{2,0,1:T(8,128)}), f32[16,128,256]{2,0,1:T(8,128)}, u32[]{:S(2)}, u32[]{:S(2)}) %all-to-all-start.1) | async-done | bytes 2097184 | tf_op jit(solution)/shard_map/all_to_all | solution.py:36
  74.8 1.9 copy.121
  76.8 0.3 copy-done.5
  77.0 2.4 convolution_bitcast_fusion.3
  79.5 1.2 copy.123
  80.7 51.3 %all_to_all.156 = f32[128,16,256]{2,1,0:T(8,128)S(1)} all-to-all(f32[128,16,256]{2,1,0:T(8,128)S(1)} %copy.123), channel_id=1, replica_groups=mesh['groups'=2,'segment'=2,'block'=8] {'block'}, dimensions={0} | all-to-all | bytes 4194304 | tf_op jit(solution)/shard_map/all_to_all | solution.py:40
  132.2 2.2 multiply_reduce_fusion.2
  134.4 8.5 %all_to_all.157 = f32[8,1,256]{2,1,0:T(1,128)S(1)} all-to-all(f32[8,1,256]{2,1,0:T(1,128)S(1)} %broadcast_in_dim.9), channel_id=1, replica_groups=mesh['groups'=2,'segment'=2,'block'=8] {'block'}, dimensions={0} | all-to-all | bytes 16384 | tf_op jit(solution)/shard_map/all_to_all | solution.py:26
  143.0 2.1 multiply_multiply_fusion.2
  145.2 1.2 fusion.12
  146.4 1.2 copy.127
  147.6 51.0 %all_to_all.158 = f32[16,128,256]{2,0,1:T(8,128)S(1)} all-to-all(f32[16,128,256]{2,0,1:T(8,128)S(1)} %copy.127), channel_id=1, replica_groups=mesh['groups'=2,'segment'=2,'block'=8] {'block'}, dimensions={1} | all-to-all | bytes 4194304 | tf_op jit(solution)/shard_map/all_to_all | solution.py:36
  198.6 0.2 copy.128
  198.9 1.3 copy-done.6
  200.2 1.2 convolution_bitcast_fusion.2
  201.4 2.6 copy.130
  204.0 5.5 %all-to-all-start.5 = ((f32[128,16,256]{2,1,0:T(8,128)}), f32[128,16,256]{2,1,0:T(8,128)S(1)}, u32[]{:S(2)}, u32[]{:S(2)}) async-start(f32[128,16,256]{2,1,0:T(8,128)} %copy.130), calls=%async_computation.5 | async-start | bytes 4194304 | tf_op jit(solution)/shard_map/all_to_all | solution.py:40
  209.5 3.0 collective-permute-start.5
  212.5 42.9 %all-to-all-done.5 = f32[128,16,256]{2,1,0:T(8,128)S(1)} async-done(((f32[128,16,256]{2,1,0:T(8,128)}), f32[128,16,256]{2,1,0:T(8,128)S(1)}, u32[]{:S(2)}, u32[]{:S(2)}) %all-to-all-start.5) | async-done | bytes 2097184 | tf_op jit(solution)/shard_map/all_to_all | solution.py:40
  255.6 1.4 copy-done
  257.0 0.9 multiply_reduce_fusion.1
  257.9 0.6 broadcast_in_dim.10
  258.5 6.1 %all-to-all-start.6 = ((f32[8,1,256]{2,1,0:T(1,128)}), f32[8,1,256]{2,1,0:T(1,128)S(1)}, u32[]{:S(2)}, u32[]{:S(2)}) async-start(f32[8,1,256]{2,1,0:T(1,128)} %broadcast_in_dim.10), calls=%async_computation.6 | async-start | bytes 16384 | tf_op jit(solution)/shard_map/all_to_all | solution.py:26
  264.6 2.6 all-to-all-done.6
  267.3 0.3 multiply_multiply_fusion.1
  267.6 1.2 copy-done.3
  268.9 1.2 fusion.9
  270.1 2.5 copy.134
  272.6 7.0 %all-to-all-start.7 = ((f32[16,128,256]{2,0,1:T(8,128)}), f32[16,128,256]{2,0,1:T(8,128)}, u32[]{:S(2)}, u32[]{:S(2)}) async-start(f32[16,128,256]{2,0,1:T(8,128)} %copy.134), calls=%async_computation.7 | async-start | bytes 4194304 | tf_op jit(solution)/shard_map/all_to_all | solution.py:36
  279.6 2.2 collective-permute-start.3
  281.8 44.6 %all-to-all-done.7 = f32[16,128,256]{2,0,1:T(8,128)} async-done(((f32[16,128,256]{2,0,1:T(8,128)}), f32[16,128,256]{2,0,1:T(8,128)}, u32[]{:S(2)}, u32[]{:S(2)}) %all-to-all-start.7) | async-done | bytes 2097184 | tf_op jit(solution)/shard_map/all_to_all | solution.py:36
  326.5 1.9 copy.135
  328.4 0.3 copy-done.7
  328.7 2.4 convolution_bitcast_fusion.1
  331.1 1.2 copy.137
  332.3 51.3 %all_to_all.159 = f32[128,16,256]{2,1,0:T(8,128)S(1)} all-to-all(f32[128,16,256]{2,1,0:T(8,128)S(1)} %copy.137), channel_id=1, replica_groups=mesh['groups'=2,'segment'=2,'block'=8] {'block'}, dimensions={0} | all-to-all | bytes 4194304 | tf_op jit(solution)/shard_map/all_to_all | solution.py:40
  383.8 2.2 multiply_reduce_fusion
  386.0 8.5 %all_to_all.160 = f32[8,1,256]{2,1,0:T(1,128)S(1)} all-to-all(f32[8,1,256]{2,1,0:T(1,128)S(1)} %broadcast_in_dim.11), channel_id=1, replica_groups=mesh['groups'=2,'segment'=2,'block'=8] {'block'}, dimensions={0} | all-to-all | bytes 16384 | tf_op jit(solution)/shard_map/all_to_all | solution.py:26
  394.6 2.1 multiply_multiply_fusion
  396.8 1.2 fusion.6
  398.0 1.2 copy.141
  399.3 50.8 %all_to_all.161 = f32[16,128,256]{2,0,1:T(8,128)S(1)} all-to-all(f32[16,128,256]{2,0,1:T(8,128)S(1)} %copy.141), channel_id=1, replica_groups=mesh['groups'=2,'segment'=2,'block'=8] {'block'}, dimensions={1} | all-to-all | bytes 4194304 | tf_op jit(solution)/shard_map/all_to_all | solution.py:36
  450.3 1.3 copy-done.8
  451.7 1.2 convolution_bitcast_fusion
  452.9 1.2 copy.144
  454.1 50.5 %all_to_all.162 = f32[128,16,256]{2,1,0:T(8,128)S(1)} all-to-all(f32[128,16,256]{2,1,0:T(8,128)S(1)} %copy.144), channel_id=1, replica_groups=mesh['groups'=2,'segment'=2,'block'=8] {'block'}, dimensions={0} | all-to-all | bytes 4194304 | tf_op jit(solution)/shard_map/all_to_all | solution.py:40
  504.8 1.4 copy-done.9
  506.2 0.7 fusion
  507.0 1.8 copy.146
  (37 shorter events, 1.5 us)
Async XLA Ops:
  0.8 12.2 %collective-permute-start.2 = (f32[2048]{0:T(1024)S(1)}, f32[2048]{0:T(1024)S(1)}, u32[]{:S(2)}, u32[]{:S(2)}) collective-permute-start(f32[2048]{0:T(1024)S(1)} %bitcast.130), channel_id=1, source_target_pairs={{8,0},{0,8},{9,1},{1,9},{10,2},{2,10},{11,3},{3,11},{12,4},{4,12},... | collective-permute-start | bytes 24584 | tf_op jit(solution)/shard_map/ppermute | solution.py:16
  4.6 11.4 %collective-permute-start.1 = (f32[16,128,128]{2,1,0:T(8,128)}, f32[16,128,128]{2,1,0:T(8,128)S(1)}, u32[]{:S(2)}, u32[]{:S(2)}) collective-permute-start(f32[16,128,128]{2,1,0:T(8,128)} %get-tuple-element.14), channel_id=1, source_target_pairs={{8,0},{0,8},{9,1},{1,9},{10,2},{2,10},{11,3},{3,11},{12,4},{4,12},... | collective-permute-start | bytes 3145736 | tf_op jit(solution)/shard_map/ppermute | solution.py:16
  7.5 8.1 %all-to-all-start = ((f32[8,1,256]{2,1,0:T(1,128)}), f32[8,1,256]{2,1,0:T(1,128)S(1)}, u32[]{:S(2)}, u32[]{:S(2)}) async-start(f32[8,1,256]{2,1,0:T(1,128)} %broadcast_in_dim.8), calls=%async_computation | async-start | bytes 16384 | tf_op jit(solution)/shard_map/all_to_all | solution.py:26
  15.6 1.6 copy-start.1
  21.0 53.8 %all-to-all-start.1 = ((f32[16,128,256]{2,0,1:T(8,128)}), f32[16,128,256]{2,0,1:T(8,128)}, u32[]{:S(2)}, u32[]{:S(2)}) async-start(f32[16,128,256]{2,0,1:T(8,128)} %copy.120), calls=%async_computation.1 | async-start | bytes 4194304 | tf_op jit(solution)/shard_map/all_to_all | solution.py:36
  31.1 45.7 %collective-permute-start = (f32[16,128,128]{2,1,0:T(8,128)}, f32[16,128,128]{2,1,0:T(8,128)}, u32[]{:S(2)}, u32[]{:S(2)}) collective-permute-start(f32[16,128,128]{2,1,0:T(8,128)} %get-tuple-element.12), channel_id=1, source_target_pairs={{8,0},{0,8},{9,1},{1,9},{10,2},{2,10},{11,3},{3,11},{12,4},{4,12},... | collective-permute-start | bytes 3145736 | tf_op jit(solution)/shard_map/ppermute | solution.py:16
  74.8 2.2 copy-start.5
  143.0 2.2 copy-start.2
  198.6 1.6 copy-start.6
  204.0 51.4 %all-to-all-start.5 = ((f32[128,16,256]{2,1,0:T(8,128)}), f32[128,16,256]{2,1,0:T(8,128)S(1)}, u32[]{:S(2)}, u32[]{:S(2)}) async-start(f32[128,16,256]{2,1,0:T(8,128)} %copy.130), calls=%async_computation.5 | async-start | bytes 4194304 | tf_op jit(solution)/shard_map/all_to_all | solution.py:40
  209.5 55.1 %collective-permute-start.5 = (f32[2048]{0:T(1024)S(1)}, f32[2048]{0:T(1024)S(1)}, u32[]{:S(2)}, u32[]{:S(2)}) collective-permute-start(f32[2048]{0:T(1024)S(1)} %bitcast.128), channel_id=1, source_target_pairs={{8,0},{0,8},{9,1},{1,9},{10,2},{2,10},{11,3},{3,11},{12,4},{4,12},... | collective-permute-start | bytes 24584 | tf_op jit(solution)/shard_map/ppermute | solution.py:16
  212.5 55.1 %collective-permute-start.4 = (f32[16,128,128]{2,1,0:T(8,128)}, f32[16,128,128]{2,1,0:T(8,128)S(1)}, u32[]{:S(2)}, u32[]{:S(2)}) collective-permute-start(f32[16,128,128]{2,1,0:T(8,128)} %get-tuple-element.13), channel_id=1, source_target_pairs={{8,0},{0,8},{9,1},{1,9},{10,2},{2,10},{11,3},{3,11},{12,4},{4,12},... | collective-permute-start | bytes 3145736 | tf_op jit(solution)/shard_map/ppermute | solution.py:16
  255.4 1.6 copy-start
  258.5 8.7 %all-to-all-start.6 = ((f32[8,1,256]{2,1,0:T(1,128)}), f32[8,1,256]{2,1,0:T(1,128)S(1)}, u32[]{:S(2)}, u32[]{:S(2)}) async-start(f32[8,1,256]{2,1,0:T(1,128)} %broadcast_in_dim.10), calls=%async_computation.6 | async-start | bytes 16384 | tf_op jit(solution)/shard_map/all_to_all | solution.py:26
  267.3 1.6 copy-start.3
  272.6 53.8 %all-to-all-start.7 = ((f32[16,128,256]{2,0,1:T(8,128)}), f32[16,128,256]{2,0,1:T(8,128)}, u32[]{:S(2)}, u32[]{:S(2)}) async-start(f32[16,128,256]{2,0,1:T(8,128)} %copy.134), calls=%async_computation.7 | async-start | bytes 4194304 | tf_op jit(solution)/shard_map/all_to_all | solution.py:36
  279.6 48.8 %collective-permute-start.3 = (f32[16,128,128]{2,1,0:T(8,128)}, f32[16,128,128]{2,1,0:T(8,128)}, u32[]{:S(2)}, u32[]{:S(2)}) collective-permute-start(f32[16,128,128]{2,1,0:T(8,128)} %get-tuple-element.11), channel_id=1, source_target_pairs={{8,0},{0,8},{9,1},{1,9},{10,2},{2,10},{11,3},{3,11},{12,4},{4,12},... | collective-permute-start | bytes 3145736 | tf_op jit(solution)/shard_map/ppermute | solution.py:16
  326.5 2.2 copy-start.7
  394.6 2.2 copy-start.4
  450.1 1.6 copy-start.8
  504.6 1.6 copy-start.9

commit v2 on v1

--- a/solution.py
+++ b/solution.py
@@ -1,7 +1,11 @@
+import functools
+
 import jax
 import jax.numpy as jnp
 from jax import lax
-from jax.sharding import PartitionSpec as P
+from jax.experimental import pallas as pl
+from jax.experimental.pallas import tpu as pltpu
+from jax.sharding import Mesh, PartitionSpec as P
 
 D = 16384
 
@@ -57,17 +61,280 @@
     return current.T
 
 
+MESH = pl.DeviceIdType.MESH
+
+
+def halves(value):
+    high = value.astype(jnp.bfloat16)
+    return high, (value - high.astype(jnp.float32)).astype(jnp.bfloat16)
+
+
+def product(weight, value):
+    wh, wl = halves(weight)
+    vh, vl = halves(value)
+    dot = functools.partial(jnp.dot, preferred_element_type=jnp.float32)
+    return dot(wh, vh) + (dot(wh, vl) + dot(wl, vh))
+
+
+def layers_kernel(
+    hi, layers, start_ref, gain_ref, right_ref, left_ref, out_ref,
+    W, N, S, A, T, M, Q,
+    wsend, wrecv, fsend, frecv, qsend, qrecv, asend, arecv, msend, mrecv,
+):
+    x = lax.axis_index("groups")
+    c = lax.axis_index("segment")
+    z = lax.axis_index("hi")
+    y = lax.axis_index("lo")
+    here = 2 * y + c
+    half = W.shape[2] // 2
+    own = pl.ds(pl.multiple_of(x * half, half), half)
+    steps = 2 * layers
+
+    def peer(d):
+        return (x, (c + d % 2) % 2, z, (y + d // 2) % 2)
+
+    barrier = pltpu.get_barrier_semaphore()
+    greeted = [(x, (c + dc) % 2, (z + dz) % hi, y) for dz in range(hi) for dc in range(2) if dz or dc]
+    greeted += [peer(2), peer(3), (1 - x, c, z, y)]
+    for device in greeted:
+        pl.semaphore_signal(barrier, inc=1, device_id=device, device_id_type=MESH)
+    pl.semaphore_wait(barrier, len(greeted))
+
+    def push_copies(step, f):
+        r = step // 4
+        source = (right_ref, left_ref)[f]
+        slot = r * 2 + f
+        for dz in range(hi):
+            zt = (z + dz) % hi
+            for dc in range(2):
+                ct = (c + dc) % 2
+                rows = pl.ds(pl.multiple_of((ct * 2 + x) * half, half), half)
+                src = source.at[r, rows]
+                dst = W.at[step, z, own]
+                if dz == 0 and dc == 0:
+                    yield pltpu.make_async_copy(src, dst, wrecv.at[step, z]), False
+                else:
+                    yield pltpu.make_async_remote_copy(
+                        src_ref=src, dst_ref=dst, send_sem=wsend.at[slot, 2 * dz + dc],
+                        recv_sem=wrecv.at[step, z], device_id=(x, ct, zt, y), device_id_type=MESH,
+                    ), True
+
+    def push(step, f):
+        @pl.when(c == (step // 2) % 2)
+        def _():
+            for copy, _ in push_copies(step, f):
+                copy.start()
+
+    def forward_copy(step, zz):
+        return pltpu.make_async_remote_copy(
+            src_ref=W.at[step, zz, own], dst_ref=W.at[step, zz, own],
+            send_sem=fsend.at[step, zz], recv_sem=frecv.at[step, zz],
+            device_id=(1 - x, c, z, y), device_id_type=MESH,
+        )
+
+    def forward(step):
+        for dz in range(hi):
+            zz = (z + dz) % hi
+            piece = W.at[step, zz, own]
+            pltpu.make_async_copy(piece, piece, wrecv.at[step, zz]).wait()
+            forward_copy(step, zz).start()
+
+    def arrived(step):
+        for zz in range(hi):
+            forward_copy(step, zz).wait_recv()
+
+    def quad_copy(kind, part, d):
+        if kind == "q":
+            src, dst, send, recv = Q.at[part, here], Q.at[part, here], qsend.at[part, d], qrecv.at[part, d]
+        else:
+            target = 2 * ((y + d // 2) % 2) + (c + d % 2) % 2
+            if kind == "a":
+                src, dst, send, recv = S.at[part, target], A.at[:, part, here], asend, arecv
+            else:
+                src, dst, send, recv = T.at[part, target], M.at[part, here], msend, mrecv
+            send, recv = send.at[part, d], recv.at[part, d]
+            if d == 0:
+                return pltpu.make_async_copy(src, dst, recv)
+        return pltpu.make_async_remote_copy(
+            src_ref=src, dst_ref=dst, send_sem=send, recv_sem=recv,
+            device_id=peer(d), device_id_type=MESH,
+        )
+
+    push(0, 0)
+    push(1, 1)
+    zero = jnp.zeros((8, 128), jnp.float32)
+
+    def start_block(b, total):
+        value = start_ref[b]
+        out_ref[b] = value
+        return total + jnp.sum((value * value).reshape(16, 8, 128), axis=0)
+
+    total = lax.fori_loop(0, hi * 8, start_block, zero)
+    forward(0)
+
+    def layer(l, total):
+        Q[l, here] = total
+        for d in (2, 3, 1):
+            quad_copy("q", l, d).start()
+        forward(2 * l + 1)
+        for d in (2, 3, 1):
+            quad_copy("q", l, d).wait()
+        everyone = Q[l, 0] + Q[l, 1] + Q[l, 2] + Q[l, 3]
+        sum_squares = jnp.sum(everyone, axis=0, keepdims=True)
+        scale = lax.rsqrt(sum_squares / D + epsilon)
+        arrived(2 * l)
+
+        @pl.when(l + 1 < layers)
+        def _():
+            push(2 * l + 2, 0)
+
+        def right_chunk(zb, carry):
+            for k in range(8):
+                b = zb * 8 + k
+                normed = out_ref[b] * scale * gain_ref[l, b]
+                N[b] = normed
+                inner = product(W[2 * l, zb, k * 128:(k + 1) * 128], normed)
+                tiles = inner.reshape(hi, 4, 8, 128)
+                for q in range(4):
+                    S[zb, q, :, k] = tiles[:, q]
+            for d in (2, 3, 1, 0):
+                quad_copy("a", zb, d).start()
+            return carry
+
+        lax.fori_loop(0, hi, right_chunk, 0)
+        arrived(2 * l + 1)
+
+        @pl.when(l + 1 < layers)
+        def _():
+            push(2 * l + 3, 1)
+
+        for part in range(hi):
+            for d in (0, 1, 2, 3):
+                quad_copy("a", part, d).wait()
+
+        def left_chunk(zj, carry):
+            flat = A.at[zj].reshape(hi * 4 * 8 * 8, 128)
+            for jj in range(8):
+                values = flat[pl.ds(jj, 128, stride=8), :]
+                mixed = product(W[2 * l + 1, zj, jj * 128:(jj + 1) * 128], values)
+                tiles = mixed.reshape(hi, 4, 8, 128)
+                for q in range(4):
+                    T[zj, q, jj] = tiles[:, q]
+            for d in (2, 3, 1, 0):
+                quad_copy("m", zj, d).start()
+            return carry
+
+        lax.fori_loop(0, hi, left_chunk, 0)
+
+        @pl.when(l + 1 < layers)
+        def _():
+            forward(2 * l + 2)
+
+        for part in range(hi):
+            for d in (0, 1, 2, 3):
+                quad_copy("m", part, d).wait()
+
+        flat = M.reshape(128 * hi * 8, 128)
+
+        def close_block(b, total):
+            mixed = flat[pl.ds(b, 128, stride=hi * 8), :]
+            normed = N[b]
+            value = out_ref[b] + mixed * (normed / (1.0 + jnp.exp(-normed)))
+            out_ref[b] = value
+            return total + jnp.sum((value * value).reshape(16, 8, 128), axis=0)
+
+        return lax.fori_loop(0, hi * 8, close_block, zero)
+
+    lax.fori_loop(0, layers, layer, total)
+    for step in range(steps):
+        @pl.when(c == (step // 2) % 2)
+        def _():
+            for copy, remote in push_copies(step, step % 2):
+                if remote:
+                    copy.wait_send()
+        for zz in range(hi):
+            forward_copy(step, zz).wait_send()
+
+
+def run_layers(current, gain_rows, rights, lefts, hi, layers):
+    f32 = jnp.float32
+    rows = rights.shape[1] // 2
+    dma = pltpu.SemaphoreType.DMA
+    vmem = pl.BlockSpec(memory_space=pltpu.VMEM)
+    anywhere = pl.BlockSpec(memory_space=pl.ANY)
+    return pl.pallas_call(
+        functools.partial(layers_kernel, hi, layers),
+        out_shape=jax.ShapeDtypeStruct(current.shape, f32),
+        in_specs=[vmem, vmem, anywhere, anywhere],
+        out_specs=vmem,
+        scratch_shapes=[
+            pltpu.VMEM((2 * layers, hi, rows, 128), f32),
+            pltpu.VMEM((hi * 8, 128, 128), f32),
+            pltpu.VMEM((hi, 4, hi, 8, 8, 128), f32),
+            pltpu.VMEM((hi, hi, 4, 8, 8, 128), f32),
+            pltpu.VMEM((hi, 4, 8, hi, 8, 128), f32),
+            pltpu.VMEM((hi, 4, 8, hi, 8, 128), f32),
+            pltpu.VMEM((layers, 4, 8, 128), f32),
+            dma((layers, 2 * hi)),
+            dma((2 * layers, hi)),
+            dma((2 * layers, hi)),
+            dma((2 * layers, hi)),
+            dma((layers, 4)),
+            dma((layers, 4)),
+            dma((hi, 4)),
+            dma((hi, 4)),
+            dma((hi, 4)),
+            dma((hi, 4)),
+        ],
+        compiler_params=pltpu.CompilerParams(
+            collective_id=0, has_side_effects=True, vmem_limit_bytes=58 * 2**20
+        ),
+    )(current, gain_rows, rights, lefts)
+
+
+def quad_body(tokens, gains, right_factors, left_factors):
+    hi = lax.axis_size("hi")
+    spread = ("segment", "hi")
+    rounds, here, size = right_factors.shape[1:4]
+    blocks = here // 2
+    rows = tokens.shape[0]
+    few = rows // hi
+    sent = tokens.reshape(hi, few, 2, blocks * size).transpose(2, 0, 1, 3)
+    rates = gains[0].reshape(rounds, 1, 2, blocks * size).transpose(2, 1, 0, 3)
+    rates = jnp.broadcast_to(rates, (2, hi, rounds, blocks * size))
+    sent = jnp.concatenate([sent, rates], axis=2).reshape(2 * hi, few + rounds, blocks * size)
+    came = lax.all_to_all(sent, spread, split_axis=0, concat_axis=0, tiled=True)
+    came = came.reshape(2, hi, few + rounds, blocks, size)
+    current = came[:, :, :few].transpose(1, 3, 4, 0, 2).reshape(hi * blocks, size, 2 * few)
+    gain_rows = came[:, :, few:].transpose(2, 0, 1, 3, 4).reshape(2 * rounds, hi * blocks, size, 1)
+    gain_rows = jnp.broadcast_to(gain_rows, (2 * rounds, hi * blocks, size, 2 * few))
+    rights = right_factors[0].swapaxes(-1, -2).reshape(rounds, here * size, size)
+    lefts = left_factors[0].swapaxes(-1, -2).reshape(rounds, here * size, size)
+    current = run_layers(current, gain_rows, rights, lefts, hi, 2 * rounds)
+    back = current.reshape(hi, blocks * size, 2, few).transpose(2, 0, 3, 1)
+    back = back.reshape(2 * hi, few, blocks * size)
+    back = lax.all_to_all(back, spread, split_axis=0, concat_axis=0, tiled=True)
+    back = back.reshape(2, hi, few, blocks * size).transpose(1, 2, 0, 3)
+    return back.reshape(rows, 2 * blocks * size)
+
+
 def solution(mesh):
+    groups, segments, devices = (mesh.shape[a] for a in ("groups", "segment", "block"))
+    if (groups, segments, devices) == (2, 2, 8):
+        finer = Mesh(mesh.devices.reshape(2, 2, 4, 2), ("groups", "segment", "hi", "lo"))
+        block, chosen = ("hi", "lo"), quad_body
+    else:
+        finer, block, chosen = mesh, "block", body
     placed = (
-        P(("groups", "segment"), "block"),
-        P("segment", None, "block"),
-        P("segment", None, "block", None, None),
-        P("segment", None, "block", None, None),
+        P(("groups", "segment"), block),
+        P("segment", None, block),
+        P("segment", None, block, None, None),
+        P("segment", None, block, None, None),
     )
     return jax.shard_map(
-        body,
-        mesh=mesh,
+        chosen,
+        mesh=finer,
         in_specs=placed,
-        out_specs=P(("groups", "segment"), "block"),
+        out_specs=P(("groups", "segment"), block),
         check_vma=False,
     )

time: 515 us -> 417 us (0.81)
  Pallas kernels: 0 us -> 281 us
  blocking collectives: 272 us -> 56.2 us
  waiting for transfers between devices: 134 us -> 33.6 us
  starting transfers between devices: 39.2 us -> 5.41 us
  matrix products: 12.1 us -> 0 us
  other arithmetic: 11.3 us -> 1 us
  local copies, waits for them, and re-layouts: 39.5 us -> 34.3 us
    pallas_call x0 -> x1, Pallas kernels: none -> 281 us  [run_layers(): pl.pallas_call(functools.partial(layers_kernel, hi, layers), out_shape=ja...]
    all_to_all x7 -> x1, blocking collectives: 272 us -> 56.2 us  [quad_body(): back = lax.all_to_all(back, spread, split_axis=0, concat_axis=0, tiled=True)]
    all_to_all x5 -> x1, waiting for transfers between devices: 134 us -> 33.6 us  [quad_body(): came = lax.all_to_all(sent, spread, split_axis=0, concat_axis=0, tiled=True)]
    all_to_all x5 -> x1, starting transfers between devices: 31.1 us -> 5.41 us  [quad_body(): came = lax.all_to_all(sent, spread, split_axis=0, concat_axis=0, tiled=True)]
    reshape x0 -> x6, local copies, waits for them, and re-layouts: none -> 12.1 us  [the longest x2 4.38 us: quad_body(): sent = tokens.reshape(hi, few, 2, blocks * size).transpose(2, 0, 1, 3)]
    dot_general x8 -> x0, matrix products: 12.1 us -> none  [the longest x4 7.27 us: apply_layer(): jnp.einsum('bjt,jbc->cjt', lax.all_to_all(inner, 'block', split_axis=1, c...]
    unnamed x21 -> x2, local copies, waits for them, and re-layouts: 10.7 us -> 2.2 us
    ppermute x6 -> x0, starting transfers between devices: 8.16 us -> none  [shifted(): return lax.ppermute(block, axis, route)]
  transfers between devices with their start and end apart: 11 -> 1, of which waited for: 5 -> 1; matrix products, arithmetic and copies ran while one was open for 3% -> 1% of each run, Pallas kernels for 0% -> 0%
where the time goes in v2:
time: 417 us; the launch traced here: 412 us
  Pallas kernels  281 us (67%)
  blocking collectives  56.2 us (13%)
  local copies, waits for them, and re-layouts  34.3 us (8%)
  waiting for transfers between devices  33.6 us (8%)
  starting transfers between devices  5.41 us (1%)
    pallas_call x1, Pallas kernels, run_layers(): pl.pallas_call(functools.partial(layers_kernel, hi, layers), out_shape=ja...  281 us
    all_to_all x1, blocking collectives, quad_body(): back = lax.all_to_all(back, spread, split_axis=0, concat_axis=0, tiled=True)  56.2 us
    all_to_all x1, waiting for transfers between devices, quad_body(): came = lax.all_to_all(sent, spread, split_axis=0, concat_axis=0, tiled=True)  33.6 us
  transfers between devices with their start and end apart: 1, of which 1 were waited for; matrix products, arithmetic and copies ran while one was open for 1% of the time, Pallas kernels for 0%

profile of v2, /device:TPU:27, one launch (start us, length us, event | category | flops | bytes accessed | tf_op | source)
XLA Modules:
  0.0 412.0 jit_solution(10061287733472995893)
XLA Ops:
  0.0 0.7 reshape_squeeze.3
  0.7 3.0 reshape.32
  3.8 1.4 copy.40
  5.2 1.0 pad_maximum_fusion
  6.2 2.7 copy.33
  8.9 5.4 %all-to-all-start = ((f32[8,66,1024]{2,1,0:T(8,128)}), f32[8,66,1024]{2,1,0:T(8,128)S(1)}, u32[]{:S(2)}, u32[]{:S(2)}) async-start(f32[8,66,1024]{2,1,0:T(8,128)} %bitcast.32), calls=%async_computation | async-start | bytes 4718592 | tf_op jit(solution)/shard_map/all_to_all | solution.py:306
  14.3 2.9 copy.27
  17.2 2.9 copy.28
  20.1 33.6 %all-to-all-done = f32[8,66,1024]{2,1,0:T(8,128)S(1)} async-done(((f32[8,66,1024]{2,1,0:T(8,128)}), f32[8,66,1024]{2,1,0:T(8,128)S(1)}, u32[]{:S(2)}, u32[]{:S(2)}) %all-to-all-start) | async-done | bytes 2162720 | tf_op jit(solution)/shard_map/all_to_all | solution.py:306
  53.7 1.5 reshape.42
  55.2 1.7 slice_bitcast_fusion
  57.0 0.4 copy.26
  57.4 0.0 slice-start
  57.4 1.8 copy.29.start_ref
  59.2 0.0 slice-done
  59.2 4.5 %broadcast_in_dim.17.gain_ref = f32[4,32,128,128]{3,2,1,0:T(8,128)} broadcast(f32[4,32,128]{2,1,0:T(8,128)S(1)} %bitcast.43), dimensions={0,1,2} | broadcast | bytes 8454144 | tf_op jit(solution)/shard_map/broadcast_in_dim | solution.py:310
  63.7 281.4 %shard_map.46 = f32[32,128,128]{2,1,0:T(8,128)} custom-call(f32[32,128,128]{2,1,0:T(8,128)} %copy.29.start_ref, f32[4,32,128,128]{3,2,1,0:T(8,128)} %broadcast_in_dim.17.gain_ref, f32[2,2048,128]{2,1,0:T(8,128)} %bitcast.39, f32[2,2048,128]{2,1,0:T(8,128)} %bitcast.40), custom_call_target="tpu_custom_call" | custom-call | tf_op jit(solution)/shard_map/pallas_call | solution.py:265
  345.1 2.4 copy.30
  347.5 1.7 reshape.38
  349.2 2.8 copy.31
  352.0 56.2 %all_to_all.10 = f32[8,64,1024]{2,1,0:T(8,128)S(1)} all-to-all(f32[8,64,1024]{2,1,0:T(8,128)S(1)} %bitcast.36), channel_id=1, replica_groups=mesh['groups'=2,'segment'=2,'hi'=4,'lo'=2] {'segment','hi'}, dimensions={0} | all-to-all | bytes 4194304 | tf_op jit(solution)/shard_map/all_to_all | solution.py:316
  408.2 1.6 copy.32
  409.8 2.2 copy.38
  (2 shorter events, 0.0 us)
Async XLA Ops:
  8.9 44.9 %all-to-all-start = ((f32[8,66,1024]{2,1,0:T(8,128)}), f32[8,66,1024]{2,1,0:T(8,128)S(1)}, u32[]{:S(2)}, u32[]{:S(2)}) async-start(f32[8,66,1024]{2,1,0:T(8,128)} %bitcast.32), calls=%async_computation | async-start | bytes 4718592 | tf_op jit(solution)/shard_map/all_to_all | solution.py:306
  57.4 1.8 slice-start

commit v3 on v2

--- a/solution.py
+++ b/solution.py
@@ -77,8 +77,9 @@
 
 
 def layers_kernel(
-    hi, layers, start_ref, gain_ref, right_ref, left_ref, out_ref,
-    W, N, S, A, T, M, Q,
+    hi, layers, token_ref, gain_ref, right_ref, left_ref, out_ref,
+    W, X, N, S, A, T, M, Q, B, G, R,
+    tsend, trecv, gsend, grecv, osend, orecv,
     wsend, wrecv, fsend, frecv, qsend, qrecv, asend, arecv, msend, mrecv,
 ):
     x = lax.axis_index("groups")
@@ -93,6 +94,8 @@
     def peer(d):
         return (x, (c + d % 2) % 2, z, (y + d // 2) % 2)
 
+    few, wide = B.shape[1] // 2, B.shape[2]
+    G[...] = jnp.zeros(G.shape, jnp.float32)
     barrier = pltpu.get_barrier_semaphore()
     greeted = [(x, (c + dc) % 2, (z + dz) % hi, y) for dz in range(hi) for dc in range(2) if dz or dc]
     greeted += [peer(2), peer(3), (1 - x, c, z, y)]
@@ -100,29 +103,48 @@
         pl.semaphore_signal(barrier, inc=1, device_id=device, device_id_type=MESH)
     pl.semaphore_wait(barrier, len(greeted))
 
+    def copy_to(src, dst, send, recv, dz, dc):
+        if dz == 0 and dc == 0:
+            return pltpu.make_async_copy(src, dst, recv)
+        return pltpu.make_async_remote_copy(
+            src_ref=src, dst_ref=dst, send_sem=send, recv_sem=recv,
+            device_id=(x, (c + dc) % 2, (z + dz) % hi, y), device_id_type=MESH,
+        )
+
+    others = [(dz, dc) for dz in range(hi) for dc in range(2)]
+
+    def token_copy(dz, dc):
+        zt, ct = (z + dz) % hi, (c + dc) % 2
+        src = token_ref.at[pl.ds(pl.multiple_of(zt * few, few), few), pl.ds(pl.multiple_of(ct * wide, wide), wide)]
+        dst = B.at[z, pl.ds(pl.multiple_of(c * few, few), few)]
+        return copy_to(src, dst, tsend.at[dz, dc], trecv.at[z, c], dz, dc)
+
+    def gain_copy(dz, dc):
+        src = gain_ref.at[:, (c + dc) % 2]
+        dst = G.at[c, :, pl.ds(pl.multiple_of(z * 8, 8), 8)]
+        return copy_to(src, dst, gsend.at[dz, dc], grecv.at[z, c], dz, dc)
+
+    def out_copy(dz, dc):
+        zt, ct = (z + dz) % hi, (c + dc) % 2
+        src = B.at[zt, pl.ds(pl.multiple_of(ct * few, few), few)]
+        dst = out_ref.at[pl.ds(pl.multiple_of(z * few, few), few), pl.ds(pl.multiple_of(c * wide, wide), wide)]
+        return copy_to(src, dst, osend.at[dz, dc], orecv.at[z, c], dz, dc)
+
     def push_copies(step, f):
         r = step // 4
         source = (right_ref, left_ref)[f]
         slot = r * 2 + f
-        for dz in range(hi):
-            zt = (z + dz) % hi
-            for dc in range(2):
-                ct = (c + dc) % 2
-                rows = pl.ds(pl.multiple_of((ct * 2 + x) * half, half), half)
-                src = source.at[r, rows]
-                dst = W.at[step, z, own]
-                if dz == 0 and dc == 0:
-                    yield pltpu.make_async_copy(src, dst, wrecv.at[step, z]), False
-                else:
-                    yield pltpu.make_async_remote_copy(
-                        src_ref=src, dst_ref=dst, send_sem=wsend.at[slot, 2 * dz + dc],
-                        recv_sem=wrecv.at[step, z], device_id=(x, ct, zt, y), device_id_type=MESH,
-                    ), True
+        for dz, dc in others:
+            rows = pl.ds(pl.multiple_of(((c + dc) % 2 * 2 + x) * half, half), half)
+            yield copy_to(
+                source.at[r, rows], W.at[step, z, own],
+                wsend.at[slot, 2 * dz + dc], wrecv.at[step, z], dz, dc,
+            )
 
     def push(step, f):
         @pl.when(c == (step // 2) % 2)
         def _():
-            for copy, _ in push_copies(step, f):
+            for copy in push_copies(step, f):
                 copy.start()
 
     def forward_copy(step, zz):
@@ -160,23 +182,40 @@
             device_id=peer(d), device_id_type=MESH,
         )
 
+    for dz, dc in others:
+        gain_copy(dz, dc).start()
+    for dz, dc in others:
+        token_copy(dz, dc).start()
     push(0, 0)
+    total = jnp.zeros((8, 128), jnp.float32)
+    for dz in range(hi):
+        zz = (z + dz) % hi
+        for cc in range(2):
+            pltpu.make_async_copy(B.at[zz, :few], B.at[zz, :few], trecv.at[zz, cc]).wait()
+            piece = G.at[cc, :, pl.ds(pl.multiple_of(zz * 8, 8), 8)]
+            pltpu.make_async_copy(piece, piece, grecv.at[zz, cc]).wait()
+        for k in range(8):
+            value = B[zz, :, k * 128:(k + 1) * 128].T
+            X[zz * 8 + k] = value
+            total = total + jnp.sum((value * value).reshape(16, 8, 128), axis=0)
     push(1, 1)
+    for dz, dc in others:
+        if dz or dc:
+            token_copy(dz, dc).wait_send()
+            gain_copy(dz, dc).wait_send()
     zero = jnp.zeros((8, 128), jnp.float32)
-
-    def start_block(b, total):
-        value = start_ref[b]
-        out_ref[b] = value
-        return total + jnp.sum((value * value).reshape(16, 8, 128), axis=0)
-
-    total = lax.fori_loop(0, hi * 8, start_block, zero)
     forward(0)
 
     def layer(l, total):
         Q[l, here] = total
         for d in (2, 3, 1):
             quad_copy("q", l, d).start()
-        forward(2 * l + 1)
+        @pl.when(l > 0)
+        def _():
+            forward(2 * l + 1)
+
+        for zb in range(hi):
+            R[zb] = G[l % 2, l // 2, zb * 8:zb * 8 + 128].T
         for d in (2, 3, 1):
             quad_copy("q", l, d).wait()
         everyone = Q[l, 0] + Q[l, 1] + Q[l, 2] + Q[l, 3]
@@ -191,7 +230,7 @@
         def right_chunk(zb, carry):
             for k in range(8):
                 b = zb * 8 + k
-                normed = out_ref[b] * scale * gain_ref[l, b]
+                normed = X[b] * scale * R[zb, :, k:k + 1]
                 N[b] = normed
                 inner = product(W[2 * l, zb, k * 128:(k + 1) * 128], normed)
                 tiles = inner.reshape(hi, 4, 8, 128)
@@ -202,6 +241,11 @@
             return carry
 
         lax.fori_loop(0, hi, right_chunk, 0)
+
+        @pl.when(l == 0)
+        def _():
+            forward(1)
+
         arrived(2 * l + 1)
 
         @pl.when(l + 1 < layers)
@@ -239,42 +283,66 @@
         def close_block(b, total):
             mixed = flat[pl.ds(b, 128, stride=hi * 8), :]
             normed = N[b]
-            value = out_ref[b] + mixed * (normed / (1.0 + jnp.exp(-normed)))
-            out_ref[b] = value
+            value = X[b] + mixed * (normed / (1.0 + jnp.exp(-normed)))
+            X[b] = value
             return total + jnp.sum((value * value).reshape(16, 8, 128), axis=0)
 
         return lax.fori_loop(0, hi * 8, close_block, zero)
 
     lax.fori_loop(0, layers, layer, total)
+    for dz in range(hi):
+        zz = (z + dz) % hi
+        for k in range(8):
+            B[zz, :, k * 128:(k + 1) * 128] = X[zz * 8 + k].T
+        for dc in range(2):
+            out_copy(dz, dc).start()
     for step in range(steps):
         @pl.when(c == (step // 2) % 2)
         def _():
-            for copy, remote in push_copies(step, step % 2):
-                if remote:
+            for i, copy in enumerate(push_copies(step, step % 2)):
+                if i:
                     copy.wait_send()
         for zz in range(hi):
             forward_copy(step, zz).wait_send()
-
-
-def run_layers(current, gain_rows, rights, lefts, hi, layers):
+    for dz, dc in others:
+        if dz or dc:
+            out_copy(dz, dc).wait_send()
+    for zz in range(hi):
+        for cc in range(2):
+            piece = out_ref.at[zz * few:(zz + 1) * few, cc * wide:(cc + 1) * wide]
+            pltpu.make_async_copy(piece, piece, orecv.at[zz, cc]).wait()
+
+
+def quad_body(tokens, gains, right_factors, left_factors):
     f32 = jnp.float32
-    rows = rights.shape[1] // 2
+    hi = lax.axis_size("hi")
+    rounds, here, size = right_factors.shape[1:4]
+    layers = 2 * rounds
+    rows = here * size // 2
+    few = tokens.shape[0] // hi
+    rates = gains[0].reshape(rounds, 2, here // 2, size)
+    rights = right_factors[0].swapaxes(-1, -2).reshape(rounds, here * size, size)
+    lefts = left_factors[0].swapaxes(-1, -2).reshape(rounds, here * size, size)
     dma = pltpu.SemaphoreType.DMA
-    vmem = pl.BlockSpec(memory_space=pltpu.VMEM)
     anywhere = pl.BlockSpec(memory_space=pl.ANY)
     return pl.pallas_call(
         functools.partial(layers_kernel, hi, layers),
-        out_shape=jax.ShapeDtypeStruct(current.shape, f32),
-        in_specs=[vmem, vmem, anywhere, anywhere],
-        out_specs=vmem,
+        out_shape=jax.ShapeDtypeStruct(tokens.shape, f32),
+        in_specs=[anywhere] * 4,
+        out_specs=anywhere,
         scratch_shapes=[
             pltpu.VMEM((2 * layers, hi, rows, 128), f32),
+            pltpu.VMEM((hi * 8, 128, 128), f32),
             pltpu.VMEM((hi * 8, 128, 128), f32),
             pltpu.VMEM((hi, 4, hi, 8, 8, 128), f32),
             pltpu.VMEM((hi, hi, 4, 8, 8, 128), f32),
             pltpu.VMEM((hi, 4, 8, hi, 8, 128), f32),
             pltpu.VMEM((hi, 4, 8, hi, 8, 128), f32),
             pltpu.VMEM((layers, 4, 8, 128), f32),
+            pltpu.VMEM((hi, 2 * few, rows), f32),
+            pltpu.VMEM((2, rounds, 128 + 8 * hi, 128), f32),
+            pltpu.VMEM((hi, 128, 128), f32),
+            *[dma((hi, 2))] * 6,
             dma((layers, 2 * hi)),
             dma((2 * layers, hi)),
             dma((2 * layers, hi)),
@@ -289,33 +357,7 @@
         compiler_params=pltpu.CompilerParams(
             collective_id=0, has_side_effects=True, vmem_limit_bytes=58 * 2**20
         ),
-    )(current, gain_rows, rights, lefts)
-
-
-def quad_body(tokens, gains, right_factors, left_factors):
-    hi = lax.axis_size("hi")
-    spread = ("segment", "hi")
-    rounds, here, size = right_factors.shape[1:4]
-    blocks = here // 2
-    rows = tokens.shape[0]
-    few = rows // hi
-    sent = tokens.reshape(hi, few, 2, blocks * size).transpose(2, 0, 1, 3)
-    rates = gains[0].reshape(rounds, 1, 2, blocks * size).transpose(2, 1, 0, 3)
-    rates = jnp.broadcast_to(rates, (2, hi, rounds, blocks * size))
-    sent = jnp.concatenate([sent, rates], axis=2).reshape(2 * hi, few + rounds, blocks * size)
-    came = lax.all_to_all(sent, spread, split_axis=0, concat_axis=0, tiled=True)
-    came = came.reshape(2, hi, few + rounds, blocks, size)
-    current = came[:, :, :few].transpose(1, 3, 4, 0, 2).reshape(hi * blocks, size, 2 * few)
-    gain_rows = came[:, :, few:].transpose(2, 0, 1, 3, 4).reshape(2 * rounds, hi * blocks, size, 1)
-    gain_rows = jnp.broadcast_to(gain_rows, (2 * rounds, hi * blocks, size, 2 * few))
-    rights = right_factors[0].swapaxes(-1, -2).reshape(rounds, here * size, size)
-    lefts = left_factors[0].swapaxes(-1, -2).reshape(rounds, here * size, size)
-    current = run_layers(current, gain_rows, rights, lefts, hi, 2 * rounds)
-    back = current.reshape(hi, blocks * size, 2, few).transpose(2, 0, 3, 1)
-    back = back.reshape(2 * hi, few, blocks * size)
-    back = lax.all_to_all(back, spread, split_axis=0, concat_axis=0, tiled=True)
-    back = back.reshape(2, hi, few, blocks * size).transpose(1, 2, 0, 3)
-    return back.reshape(rows, 2 * blocks * size)
+    )(tokens, rates, rights, lefts)
 
 
 def solution(mesh):

time: 417 us -> 370 us (0.89); the launches traced: 412 us -> 370 us
  Pallas kernels: 281 us -> 360 us
  blocking collectives: 56.2 us -> 0 us
  waiting for transfers between devices: 33.6 us -> 0 us
  local copies, waits for them, and re-layouts: 34.3 us -> 9.35 us
  starting transfers between devices: 5.41 us -> 0 us
    pallas_call x1, Pallas kernels: 281 us -> 360 us  [quad_body(): pl.pallas_call(functools.partial(layers_kernel, hi, layers), out_shape=ja...]
    all_to_all x1 -> x0, blocking collectives: 56.2 us -> none  [quad_body(): back = lax.all_to_all(back, spread, split_axis=0, concat_axis=0, tiled=True)]
    all_to_all x1 -> x0, waiting for transfers between devices: 33.6 us -> none  [quad_body(): came = lax.all_to_all(sent, spread, split_axis=0, concat_axis=0, tiled=True)]
    reshape x6 -> x0, local copies, waits for them, and re-layouts: 12.1 us -> none  [the longest x2 4.38 us: quad_body(): sent = tokens.reshape(hi, few, 2, blocks * size).transpose(2, 0, 1, 3)]
    transpose x4 -> x0, local copies, waits for them, and re-layouts: 6.54 us -> none  [the longest x1 2.81 us: quad_body(): back = current.reshape(hi, blocks * size, 2, few).transpose(2, 0, 3, 1)]
    all_to_all x1 -> x0, starting transfers between devices: 5.41 us -> none  [quad_body(): came = lax.all_to_all(sent, spread, split_axis=0, concat_axis=0, tiled=True)]
    broadcast_in_dim x2 -> x0, local copies, waits for them, and re-layouts: 4.54 us -> none  [the longest x1 4.53 us: quad_body(): jnp.broadcast_to(gain_rows, (2 * rounds, hi * blocks, size, 2 * few))]
  transfers between devices with their start and end apart: 1 -> 0, of which waited for: 1 -> 0; matrix products, arithmetic and copies ran while one was open for 1% -> 0% of each run, Pallas kernels for 0% -> 0%
where the time goes in v3:
time: 370 us
  Pallas kernels  360 us (97%)
  local copies, waits for them, and re-layouts  9.35 us (3%)
    pallas_call x1, Pallas kernels, quad_body(): pl.pallas_call(functools.partial(layers_kernel, hi, layers), out_shape=ja...  360 us

profile of v3, /device:TPU:27, one launch (start us, length us, event | category | flops | bytes accessed | tf_op | source)
XLA Modules:
  0.0 369.6 jit_solution(1029711610071043747)
XLA Ops:
  0.0 1.3 copy.9
  1.3 0.0 copy-start
  1.3 3.0 copy.5
  4.3 0.0 copy-done
  4.4 1.9 copy.6
  6.2 360.3 %shard_map.46 = f32[256,2048]{1,0:T(8,128)} custom-call(f32[256,2048]{1,0:T(8,128)} %token_ref.1, f32[2,2,8,128]{3,2,1,0:T(8,128)} %bitcast.18, f32[2,2048,128]{2,1,0:T(8,128)} %bitcast.14, f32[2,2048,128]{2,1,0:T(8,128)} %bitcast.15), custom_call_target="tpu_custom_call" | custom-call | tf_op jit(solution)/shard_map/pallas_call | solution.py:328
  366.5 3.1 copy.11
Async XLA Ops:
  1.3 3.0 copy-start

commit v4 on v3

--- a/solution.py
+++ b/solution.py
@@ -121,7 +121,7 @@
 
     def gain_copy(dz, dc):
         src = gain_ref.at[:, (c + dc) % 2]
-        dst = G.at[c, :, pl.ds(pl.multiple_of(z * 8, 8), 8)]
+        dst = G.at[c, z, :, :8]
         return copy_to(src, dst, gsend.at[dz, dc], grecv.at[z, c], dz, dc)
 
     def out_copy(dz, dc):
@@ -130,11 +130,11 @@
         dst = out_ref.at[pl.ds(pl.multiple_of(z * few, few), few), pl.ds(pl.multiple_of(c * wide, wide), wide)]
         return copy_to(src, dst, osend.at[dz, dc], orecv.at[z, c], dz, dc)
 
-    def push_copies(step, f):
+    def push_copies(step, f, chosen=others):
         r = step // 4
         source = (right_ref, left_ref)[f]
         slot = r * 2 + f
-        for dz, dc in others:
+        for dz, dc in chosen:
             rows = pl.ds(pl.multiple_of(((c + dc) % 2 * 2 + x) * half, half), half)
             yield copy_to(
                 source.at[r, rows], W.at[step, z, own],
@@ -154,12 +154,14 @@
             device_id=(1 - x, c, z, y), device_id_type=MESH,
         )
 
+    def forward_from(step, zz):
+        piece = W.at[step, zz, own]
+        pltpu.make_async_copy(piece, piece, wrecv.at[step, zz]).wait()
+        forward_copy(step, zz).start()
+
     def forward(step):
         for dz in range(hi):
-            zz = (z + dz) % hi
-            piece = W.at[step, zz, own]
-            pltpu.make_async_copy(piece, piece, wrecv.at[step, zz]).wait()
-            forward_copy(step, zz).start()
+            forward_from(step, (z + dz) % hi)
 
     def arrived(step):
         for zz in range(hi):
@@ -182,76 +184,79 @@
             device_id=peer(d), device_id_type=MESH,
         )
 
+    def squares(value):
+        return jnp.sum((value * value).reshape(16, 8, 128), axis=0)
+
+    def right_block(l, zb, k, value):
+        scaled = value * R[zb, :, k:k + 1]
+        N[zb * 8 + k] = scaled
+        inner = product(W[2 * l, zb, k * 128:(k + 1) * 128], scaled)
+        tiles = inner.reshape(hi, 4, 8, 128)
+        for q in range(4):
+            S[zb, q, :, k] = tiles[:, q]
+
+    def send_right(zb):
+        for d in (2, 3, 1, 0):
+            quad_copy("a", zb, d).start()
+
+    def send_squares(l, total):
+        Q[l, here] = total
+        for d in (2, 3, 1):
+            quad_copy("q", l, d).start()
+
     for dz, dc in others:
         gain_copy(dz, dc).start()
-    for dz, dc in others:
-        token_copy(dz, dc).start()
-    push(0, 0)
-    total = jnp.zeros((8, 128), jnp.float32)
+    for dz in range(hi):
+        for dc in range(2):
+            token_copy(dz, dc).start()
+
+        @pl.when(c == 0)
+        def _():
+            for copy in push_copies(0, 0, others[2 * dz:2 * dz + 2]):
+                copy.start()
+
+    zero = jnp.zeros((8, 128), jnp.float32)
+    total = zero
     for dz in range(hi):
         zz = (z + dz) % hi
         for cc in range(2):
-            pltpu.make_async_copy(B.at[zz, :few], B.at[zz, :few], trecv.at[zz, cc]).wait()
-            piece = G.at[cc, :, pl.ds(pl.multiple_of(zz * 8, 8), 8)]
+            piece = B.at[zz, cc * few:(cc + 1) * few]
+            pltpu.make_async_copy(piece, piece, trecv.at[zz, cc]).wait()
+            piece = G.at[cc, zz, :, :8]
             pltpu.make_async_copy(piece, piece, grecv.at[zz, cc]).wait()
         for k in range(8):
             value = B[zz, :, k * 128:(k + 1) * 128].T
             X[zz * 8 + k] = value
-            total = total + jnp.sum((value * value).reshape(16, 8, 128), axis=0)
+            total = total + squares(value)
+        forward_from(0, zz)
+    send_squares(0, total)
     push(1, 1)
+
+    def first_chunk(dz, carry):
+        zz = lax.rem(z + dz, hi)
+        R[zz] = G[0, zz, 0].T
+        forward_copy(0, zz).wait_recv()
+        for k in range(8):
+            right_block(0, zz, k, X[zz * 8 + k])
+        send_right(zz)
+        return carry
+
+    lax.fori_loop(0, hi, first_chunk, 0)
     for dz, dc in others:
         if dz or dc:
             token_copy(dz, dc).wait_send()
             gain_copy(dz, dc).wait_send()
-    zero = jnp.zeros((8, 128), jnp.float32)
-    forward(0)
-
-    def layer(l, total):
-        Q[l, here] = total
-        for d in (2, 3, 1):
-            quad_copy("q", l, d).start()
-        @pl.when(l > 0)
-        def _():
-            forward(2 * l + 1)
-
-        for zb in range(hi):
-            R[zb] = G[l % 2, l // 2, zb * 8:zb * 8 + 128].T
+
+    def layer(l, last):
         for d in (2, 3, 1):
             quad_copy("q", l, d).wait()
         everyone = Q[l, 0] + Q[l, 1] + Q[l, 2] + Q[l, 3]
         sum_squares = jnp.sum(everyone, axis=0, keepdims=True)
         scale = lax.rsqrt(sum_squares / D + epsilon)
-        arrived(2 * l)
-
-        @pl.when(l + 1 < layers)
-        def _():
+        forward(2 * l + 1)
+        arrived(2 * l + 1)
+        if not last:
             push(2 * l + 2, 0)
-
-        def right_chunk(zb, carry):
-            for k in range(8):
-                b = zb * 8 + k
-                normed = X[b] * scale * R[zb, :, k:k + 1]
-                N[b] = normed
-                inner = product(W[2 * l, zb, k * 128:(k + 1) * 128], normed)
-                tiles = inner.reshape(hi, 4, 8, 128)
-                for q in range(4):
-                    S[zb, q, :, k] = tiles[:, q]
-            for d in (2, 3, 1, 0):
-                quad_copy("a", zb, d).start()
-            return carry
-
-        lax.fori_loop(0, hi, right_chunk, 0)
-
-        @pl.when(l == 0)
-        def _():
-            forward(1)
-
-        arrived(2 * l + 1)
-
-        @pl.when(l + 1 < layers)
-        def _():
-            push(2 * l + 3, 1)
-
         for part in range(hi):
             for d in (0, 1, 2, 3):
                 quad_copy("a", part, d).wait()
@@ -259,7 +264,7 @@
         def left_chunk(zj, carry):
             flat = A.at[zj].reshape(hi * 4 * 8 * 8, 128)
             for jj in range(8):
-                values = flat[pl.ds(jj, 128, stride=8), :]
+                values = flat[pl.ds(jj, 128, stride=8), :] * scale
                 mixed = product(W[2 * l + 1, zj, jj * 128:(jj + 1) * 128], values)
                 tiles = mixed.reshape(hi, 4, 8, 128)
                 for q in range(4):
@@ -269,33 +274,48 @@
             return carry
 
         lax.fori_loop(0, hi, left_chunk, 0)
-
-        @pl.when(l + 1 < layers)
-        def _():
+        if not last:
+            push(2 * l + 3, 1)
             forward(2 * l + 2)
-
         for part in range(hi):
             for d in (0, 1, 2, 3):
                 quad_copy("m", part, d).wait()
-
         flat = M.reshape(128 * hi * 8, 128)
 
-        def close_block(b, total):
+        def closed(b):
             mixed = flat[pl.ds(b, 128, stride=hi * 8), :]
-            normed = N[b]
-            value = X[b] + mixed * (normed / (1.0 + jnp.exp(-normed)))
-            X[b] = value
-            return total + jnp.sum((value * value).reshape(16, 8, 128), axis=0)
-
-        return lax.fori_loop(0, hi * 8, close_block, zero)
-
-    lax.fori_loop(0, layers, layer, total)
-    for dz in range(hi):
-        zz = (z + dz) % hi
-        for k in range(8):
-            B[zz, :, k * 128:(k + 1) * 128] = X[zz * 8 + k].T
-        for dc in range(2):
-            out_copy(dz, dc).start()
+            normed = N[b] * scale
+            return X[b] + mixed * (normed / (1.0 + jnp.exp(-normed)))
+
+        if last:
+            for dz in range(hi):
+                zz = (z + dz) % hi
+                for k in range(8):
+                    B[zz, :, k * 128:(k + 1) * 128] = closed(zz * 8 + k).T
+                for dc in range(2):
+                    out_copy(dz, dc).start()
+            return
+        arrived(2 * l + 2)
+
+        def next_chunk(dz, total):
+            zb = lax.rem(z + dz, hi)
+            R[zb] = G[(l + 1) % 2, zb, (l + 1) // 2].T
+            for k in range(8):
+                value = closed(zb * 8 + k)
+                X[zb * 8 + k] = value
+                total = total + squares(value)
+                right_block(l + 1, zb, k, value)
+            send_right(zb)
+            return total
+
+        send_squares(l + 1, lax.fori_loop(0, hi, next_chunk, zero))
+
+    def inner_layer(l, carry):
+        layer(l, False)
+        return carry
+
+    lax.fori_loop(0, layers - 1, inner_layer, 0)
+    layer(layers - 1, True)
     for step in range(steps):
         @pl.when(c == (step // 2) % 2)
         def _():
@@ -340,7 +360,7 @@
             pltpu.VMEM((hi, 4, 8, hi, 8, 128), f32),
             pltpu.VMEM((layers, 4, 8, 128), f32),
             pltpu.VMEM((hi, 2 * few, rows), f32),
-            pltpu.VMEM((2, rounds, 128 + 8 * hi, 128), f32),
+            pltpu.VMEM((2, hi, rounds, 128, 128), f32),
             pltpu.VMEM((hi, 128, 128), f32),
             *[dma((hi, 2))] * 6,
             dma((layers, 2 * hi)),

time: 370 us -> 468 us (1.26)
  Pallas kernels: 360 us -> 454 us
    pallas_call x1, Pallas kernels: 360 us -> 454 us  [quad_body(): pl.pallas_call(functools.partial(layers_kernel, hi, layers), out_shape=ja...]
where the time goes in v4:
time: 468 us; the launch traced here: 463 us
  Pallas kernels  454 us (97%)
  local copies, waits for them, and re-layouts  9.35 us (2%)
    pallas_call x1, Pallas kernels, quad_body(): pl.pallas_call(functools.partial(layers_kernel, hi, layers), out_shape=ja...  454 us

profile of v4, /device:TPU:27, one launch (start us, length us, event | category | flops | bytes accessed | tf_op | source)
XLA Modules:
  0.0 463.4 jit_solution(15692015414562839211)
XLA Ops:
  0.0 1.3 copy.9
  1.3 0.0 copy-start
  1.3 3.0 copy.5
  4.3 0.0 copy-done
  4.4 1.9 copy.6
  6.2 454.1 %shard_map.46 = f32[256,2048]{1,0:T(8,128)} custom-call(f32[256,2048]{1,0:T(8,128)} %token_ref.1, f32[2,2,8,128]{3,2,1,0:T(8,128)} %bitcast.18, f32[2,2048,128]{2,1,0:T(8,128)} %bitcast.14, f32[2,2048,128]{2,1,0:T(8,128)} %bitcast.15), custom_call_target="tpu_custom_call" | custom-call | tf_op jit(solution)/shard_map/pallas_call | solution.py:348
  460.3 3.1 copy.11
Async XLA Ops:
  1.3 3.0 copy-start

commit v5 on v4

--- a/solution.py
+++ b/solution.py
@@ -147,6 +147,13 @@
             for copy in push_copies(step, f):
                 copy.start()
 
+    def push_some(step, f, dz):
+        for i in range(hi):
+            @pl.when((dz == i) & (step < steps) & (c == (step // 2) % 2))
+            def _():
+                for copy in push_copies(step, f, others[2 * i:2 * i + 2]):
+                    copy.start()
+
     def forward_copy(step, zz):
         return pltpu.make_async_remote_copy(
             src_ref=W.at[step, zz, own], dst_ref=W.at[step, zz, own],
@@ -239,6 +246,7 @@
         for k in range(8):
             right_block(0, zz, k, X[zz * 8 + k])
         send_right(zz)
+        push_some(2, 0, dz)
         return carry
 
     lax.fori_loop(0, hi, first_chunk, 0)
@@ -253,13 +261,17 @@
         everyone = Q[l, 0] + Q[l, 1] + Q[l, 2] + Q[l, 3]
         sum_squares = jnp.sum(everyone, axis=0, keepdims=True)
         scale = lax.rsqrt(sum_squares / D + epsilon)
-        forward(2 * l + 1)
+        if not last:
+            @pl.when(l == 0)
+            def _():
+                forward(1)
         arrived(2 * l + 1)
-        if not last:
-            push(2 * l + 2, 0)
         for part in range(hi):
             for d in (0, 1, 2, 3):
                 quad_copy("a", part, d).wait()
+
+        if not last:
+            forward(2 * l + 2)
 
         def left_chunk(zj, carry):
             flat = A.at[zj].reshape(hi * 4 * 8 * 8, 128)
@@ -271,12 +283,11 @@
                     T[zj, q, jj] = tiles[:, q]
             for d in (2, 3, 1, 0):
                 quad_copy("m", zj, d).start()
+            if not last:
+                push_some(2 * l + 3, 1, zj)
             return carry
 
         lax.fori_loop(0, hi, left_chunk, 0)
-        if not last:
-            push(2 * l + 3, 1)
-            forward(2 * l + 2)
         for part in range(hi):
             for d in (0, 1, 2, 3):
                 quad_copy("m", part, d).wait()
@@ -296,6 +307,7 @@
                     out_copy(dz, dc).start()
             return
         arrived(2 * l + 2)
+        forward(2 * l + 3)
 
         def next_chunk(dz, total):
             zb = lax.rem(z + dz, hi)
@@ -306,6 +318,7 @@
                 total = total + squares(value)
                 right_block(l + 1, zb, k, value)
             send_right(zb)
+            push_some(2 * l + 4, 0, dz)
             return total
 
         send_squares(l + 1, lax.fori_loop(0, hi, next_chunk, zero))

time: 468 us -> 371 us (0.79)
  Pallas kernels: 454 us -> 360 us
    pallas_call x1, Pallas kernels: 454 us -> 360 us  [quad_body(): pl.pallas_call(functools.partial(layers_kernel, hi, layers), out_shape=ja...]
where the time goes in v5:
time: 371 us; the launch traced here: 369 us
  Pallas kernels  360 us (97%)
  local copies, waits for them, and re-layouts  9.35 us (3%)
    pallas_call x1, Pallas kernels, quad_body(): pl.pallas_call(functools.partial(layers_kernel, hi, layers), out_shape=ja...  360 us

profile of v5, /device:TPU:27, one launch (start us, length us, event | category | flops | bytes accessed | tf_op | source)
XLA Modules:
  0.0 369.4 jit_solution(10640873890135827434)
XLA Ops:
  0.0 1.3 copy.9
  1.3 0.0 copy-start
  1.3 3.0 copy.5
  4.3 0.0 copy-done
  4.4 1.9 copy.6
  6.2 360.1 %shard_map.46 = f32[256,2048]{1,0:T(8,128)} custom-call(f32[256,2048]{1,0:T(8,128)} %token_ref.1, f32[2,2,8,128]{3,2,1,0:T(8,128)} %bitcast.18, f32[2,2048,128]{2,1,0:T(8,128)} %bitcast.14, f32[2,2048,128]{2,1,0:T(8,128)} %bitcast.15), custom_call_target="tpu_custom_call" | custom-call | tf_op jit(solution)/shard_map/pallas_call | solution.py:361
  366.3 3.1 copy.11
Async XLA Ops:
  1.3 3.0 copy-start
